TPU v7x, 32 devices: a whole 2x2x4 slice. The times are simulated.
32 devices in a mesh: rows: 8 (over z, x), seq: 4 (over y, core).
Axes of the slice: x: 2, y: 2, z: 4, core: 2. Of those that a mesh axis runs over, the one named last changes fastest.
Arguments:
- inputs: bfloat16 [8, 2048, 1024], P('rows', 'seq'), may hold values from -6 to 6
- skip_feats: bfloat16 [8, 2048, 1024], P('rows', 'seq'), may hold values from -6 to 6
- seg_ids: int32 [8, 2048], P('rows'), may hold values from 0 to 5, never falling along the last dimension, each value on 1 to 682 neighbouring positions
- frame_valid: int32 [8, 2048], P('rows'), may hold values 0 or 1
- w_skip: bfloat16 [2048, 1024], replicated, may hold values from -0.125 to 0.125
- gain_one: bfloat16 [1024], replicated, may hold values from 0.5 to 1.5
- w_qkv: bfloat16 [1024, 3072], replicated, may hold values from -0.1875 to 0.1875
- w_out: bfloat16 [1024, 1024], replicated, may hold values from -0.5 to 0.5
- gain_two: bfloat16 [1024], replicated, may hold values from 0.5 to 1.5
- w_up: bfloat16 [1024, 4096], replicated, may hold values from -0.1875 to 0.1875
- b_up: bfloat16 [4096], replicated, may hold values from -3 to 3
- w_down: bfloat16 [4096, 1024], replicated, may hold values from -0.09375 to 0.09375
- b_down: bfloat16 [1024], replicated, may hold values from -2 to 2
- cotangent: bfloat16 [8, 2048, 1024], P('rows', 'seq'), may hold values from -6 to 6
Outputs:
- output: bfloat16 [8, 2048, 1024], P('rows', 'seq')
- input_grad: bfloat16 [8, 2048, 1024], P('rows', 'seq')
- skip_grad: bfloat16 [8, 2048, 1024], P('rows', 'seq')
- w_skip_grad: float32 [2048, 1024], P(('rows', 'seq'))
- gain_one_grad: float32 [1024], P(('rows', 'seq'))
- w_qkv_grad: float32 [1024, 3072], P(('rows', 'seq'))
- w_out_grad: float32 [1024, 1024], P(('rows', 'seq'))
- gain_two_grad: float32 [1024], P(('rows', 'seq'))
- w_up_grad: float32 [1024, 4096], P(('rows', 'seq'))
- b_up_grad: float32 [4096], P(('rows', 'seq'))
- w_down_grad: float32 [4096, 1024], P(('rows', 'seq'))
- b_down_grad: float32 [1024], P(('rows', 'seq'))
Inputs may be any that keep to these rules, and one draw needn't show every extreme that they name: `seg_ids`: in each row the segment numbers never fall along the frames; every segment has 1 to 682 frames and one has exactly 682.
All inputs are finite; a program needn't handle non-finite values. No bound on the sum of `frame_valid` on one device may be relied on, other than what follows from the above.
Results may differ from a plain program's by a relative error of at most 0.015.
Values may be sent and summed in bfloat16 or wider, within the bound.
A program may use at most 192 MiB of HBM per device.

v0:
```python
import math
import jax
import jax.numpy as jnp
from jax import lax
from jax.sharding import PartitionSpec as P

D = 1024
H = 16
HD = 64
epsilon = 1e-05


def norm_forward(value, gain_vec):
    center = value - jnp.mean(value, axis=-1, keepdims=True)
    spread = jnp.mean(center * center, axis=-1, keepdims=True)
    inverse = lax.rsqrt(spread + epsilon)
    unit = center * inverse
    return (unit, inverse, unit * gain_vec)


def norm_backward(upstream, unit, inverse, gain_vec):
    scaled = upstream * gain_vec
    gain_grad = jnp.sum(upstream * unit, axis=(0, 1))
    inner = (
        scaled
        - jnp.mean(scaled, axis=-1, keepdims=True)
        - unit * jnp.mean(scaled * unit, axis=-1, keepdims=True)
    )
    return (inverse * inner, gain_grad)


def gelu_exact(value):
    return jax.nn.gelu(value, approximate=False)


def block_scores(q_blk, pos_blk, seg_blk, all_keys, seg_row, valid_row, slopes, score_scale):
    key_pos = jnp.arange(all_keys.shape[0])
    scores = (
        jnp.einsum("qhd,khd->hqk", q_blk, all_keys, preferred_element_type=jnp.float32)
        * score_scale
    )
    distance = jnp.abs(pos_blk[:, None] - key_pos[None, :]).astype(jnp.float32)
    scores = scores - slopes[:, None, None] * distance[None]
    allowed = (seg_blk[:, None] == seg_row[None, :]) & (
        (valid_row[None, :] == 1) | (pos_blk[:, None] == key_pos[None, :])
    )
    return jnp.where(allowed[None], scores, -jnp.inf)


def split_row(packed_row, heads_local):
    length = packed_row.shape[0]
    qkv_rows = packed_row.reshape(length, 3, heads_local, HD)
    return (qkv_rows[:, 0], qkv_rows[:, 1], qkv_rows[:, 2])


def attend_row(packed_row, seg_row, valid_row, slopes, heads_local, block_rows, score_scale):
    length = packed_row.shape[0]
    queries, all_keys, all_values = split_row(packed_row, heads_local)
    count = length // block_rows
    positions = jnp.arange(length)

    def one_block(block_in):
        q_blk, pos_blk, seg_blk = block_in
        scores = block_scores(
            q_blk, pos_blk, seg_blk, all_keys, seg_row, valid_row, slopes, score_scale
        )
        peak = jnp.max(scores, axis=-1, keepdims=True)
        log_total = peak + jnp.log(jnp.sum(jnp.exp(scores - peak), axis=-1, keepdims=True))
        attn_probs = jnp.exp(scores - log_total).astype(jnp.bfloat16)
        attended = jnp.einsum(
            "hqk,khd->qhd", attn_probs, all_values, preferred_element_type=jnp.float32
        )
        return (attended.astype(jnp.bfloat16), log_total[..., 0])

    attended, log_total = lax.map(
        one_block,
        (
            queries.reshape(count, block_rows, heads_local, HD),
            positions.reshape(count, block_rows),
            seg_row.reshape(count, block_rows),
        ),
    )
    return (attended.reshape(length, 1, heads_local * HD), log_total)


def attend_row_back(
    packed_row,
    log_total,
    grad_row,
    seg_row,
    valid_row,
    slopes,
    heads_local,
    block_rows,
    score_scale,
):
    length = packed_row.shape[0]
    queries, all_keys, all_values = split_row(packed_row, heads_local)
    count = length // block_rows
    positions = jnp.arange(length)
    grad_out = grad_row.reshape(count, block_rows, heads_local, HD)

    def one_block(carry, block_in):
        key_grad, value_grad = carry
        q_blk, pos_blk, seg_blk, total_blk, grad_blk = block_in
        scores = block_scores(
            q_blk, pos_blk, seg_blk, all_keys, seg_row, valid_row, slopes, score_scale
        )
        soft = jnp.exp(scores - total_blk[..., None])
        value_grad = value_grad + jnp.einsum(
            "hqk,qhd->khd", soft.astype(jnp.bfloat16), grad_blk, preferred_element_type=jnp.float32
        )
        prob_grad = jnp.einsum(
            "qhd,khd->hqk", grad_blk, all_values, preferred_element_type=jnp.float32
        )
        score_grad = (
            soft * (prob_grad - jnp.sum(soft * prob_grad, axis=-1, keepdims=True))
        ).astype(jnp.bfloat16)
        query_grad = (
            jnp.einsum("hqk,khd->qhd", score_grad, all_keys, preferred_element_type=jnp.float32)
            * score_scale
        )
        key_grad = (
            key_grad
            + jnp.einsum("hqk,qhd->khd", score_grad, q_blk, preferred_element_type=jnp.float32)
            * score_scale
        )
        return ((key_grad, value_grad), query_grad)

    zero_rows = jnp.zeros((length, heads_local, HD), jnp.float32)
    (key_grad, value_grad), query_grad = lax.scan(
        one_block,
        (zero_rows, zero_rows),
        (
            queries.reshape(count, block_rows, heads_local, HD),
            positions.reshape(count, block_rows),
            seg_row.reshape(count, block_rows),
            log_total,
            grad_out,
        ),
    )
    stacked = jnp.stack([query_grad.reshape(length, heads_local, HD), key_grad, value_grad], axis=1)
    return stacked.astype(jnp.bfloat16).reshape(length, 3, 1, heads_local * HD)


def body(
    inputs,
    skip_feats,
    seg_ids,
    frame_valid,
    w_skip,
    gain_one,
    w_qkv,
    w_out,
    gain_two,
    w_up,
    b_up,
    w_down,
    b_down,
    cotangent,
):
    parts = lax.axis_size("seq")
    heads_local = H // parts
    width_local = heads_local * HD
    rows_here = inputs.shape[0]
    frames = inputs.shape[1]
    length = frames * parts
    block_rows = min(512, length)
    score_scale = 1.0 / math.sqrt(HD)
    first_head = lax.axis_index("seq") * heads_local
    slopes = jnp.exp2(-8.0 * (first_head + jnp.arange(heads_local) + 1).astype(jnp.float32) / H)
    gain_first = gain_one.astype(jnp.float32)
    gain_second = gain_two.astype(jnp.float32)
    bias_up = b_up.astype(jnp.float32)
    joined = jnp.concatenate([inputs, skip_feats], axis=-1)
    stem_out = jnp.einsum("rfc,cd->rfd", joined, w_skip, preferred_element_type=jnp.float32)
    unit_one, inverse_one, normed = norm_forward(stem_out, gain_first)
    normed = normed.astype(jnp.bfloat16)
    packed = jnp.einsum("rfd,de->rfe", normed, w_qkv, preferred_element_type=jnp.float32).astype(
        jnp.bfloat16
    )
    packed = packed.reshape(rows_here, frames, 3, parts, width_local)
    by_heads = lax.all_to_all(packed, "seq", split_axis=3, concat_axis=1, tiled=True)

    def forward_row(row_data):
        return attend_row(
            row_data[0], row_data[1], row_data[2], slopes, heads_local, block_rows, score_scale
        )

    attended, log_total = lax.map(forward_row, (by_heads, seg_ids, frame_valid))
    by_frames = lax.all_to_all(attended, "seq", split_axis=1, concat_axis=2, tiled=True)
    mixed_out = by_frames.reshape(rows_here, frames, D)
    middle = stem_out + jnp.einsum(
        "rfd,de->rfe", mixed_out, w_out, preferred_element_type=jnp.float32
    )
    unit_two, inverse_two, second = norm_forward(middle, gain_second)
    second = second.astype(jnp.bfloat16)
    hidden = jnp.einsum("rfd,dk->rfk", second, w_up, preferred_element_type=jnp.float32) + bias_up
    active_full, gelu_back = jax.vjp(gelu_exact, hidden)
    active = active_full.astype(jnp.bfloat16)
    result = (
        middle
        + jnp.einsum("rfk,kd->rfd", active, w_down, preferred_element_type=jnp.float32)
        + b_down.astype(jnp.float32)
    )
    output = result.astype(jnp.bfloat16)
    cot_full = cotangent.astype(jnp.float32)
    down_grad = jnp.einsum("rfk,rfd->kd", active, cotangent, preferred_element_type=jnp.float32)
    bias_down_grad = jnp.sum(cot_full, axis=(0, 1))
    active_grad = jnp.einsum("rfd,kd->rfk", cotangent, w_down, preferred_element_type=jnp.float32)
    hidden_grad = gelu_back(active_grad)[0].astype(jnp.bfloat16)
    up_grad = jnp.einsum("rfd,rfk->dk", second, hidden_grad, preferred_element_type=jnp.float32)
    bias_up_grad = jnp.sum(hidden_grad.astype(jnp.float32), axis=(0, 1))
    second_grad = jnp.einsum("rfk,dk->rfd", hidden_grad, w_up, preferred_element_type=jnp.float32)
    middle_part, gain_two_grad = norm_backward(second_grad, unit_two, inverse_two, gain_second)
    middle_grad = cot_full + middle_part
    middle_low = middle_grad.astype(jnp.bfloat16)
    out_grad = jnp.einsum("rfd,rfe->de", mixed_out, middle_low, preferred_element_type=jnp.float32)
    mixed_grad = jnp.einsum(
        "rfe,de->rfd", middle_low, w_out, preferred_element_type=jnp.float32
    ).astype(jnp.bfloat16)
    grad_heads = lax.all_to_all(
        mixed_grad.reshape(rows_here, frames, parts, width_local),
        "seq",
        split_axis=2,
        concat_axis=1,
        tiled=True,
    )

    def backward_row(row_data):
        return attend_row_back(
            row_data[0],
            row_data[1],
            row_data[2],
            row_data[3],
            row_data[4],
            slopes,
            heads_local,
            block_rows,
            score_scale,
        )

    packed_grad = lax.map(backward_row, (by_heads, log_total, grad_heads, seg_ids, frame_valid))
    packed_back = lax.all_to_all(packed_grad, "seq", split_axis=1, concat_axis=3, tiled=True)
    packed_back = packed_back.reshape(rows_here, frames, 3 * D)
    qkv_grad = jnp.einsum("rfd,rfe->de", normed, packed_back, preferred_element_type=jnp.float32)
    normed_grad = jnp.einsum("rfe,de->rfd", packed_back, w_qkv, preferred_element_type=jnp.float32)
    stem_part, gain_one_grad = norm_backward(normed_grad, unit_one, inverse_one, gain_first)
    stem_low = (middle_grad + stem_part).astype(jnp.bfloat16)
    skip_w_grad = jnp.einsum("rfc,rfd->cd", joined, stem_low, preferred_element_type=jnp.float32)
    joined_grad = jnp.einsum("rfd,cd->rfc", stem_low, w_skip, preferred_element_type=jnp.float32)
    input_grad = joined_grad[..., :D].astype(jnp.bfloat16)
    skip_grad = joined_grad[..., D:].astype(jnp.bfloat16)
    (
        skip_share,
        gain_one_share,
        qkv_share,
        out_share,
        gain_two_share,
        up_share,
        bias_up_share,
        down_share,
        bias_down_share,
    ) = (
        lax.psum_scatter(skip_w_grad, ("rows", "seq"), scatter_dimension=0, tiled=True),
        lax.psum_scatter(gain_one_grad, ("rows", "seq"), scatter_dimension=0, tiled=True),
        lax.psum_scatter(qkv_grad, ("rows", "seq"), scatter_dimension=0, tiled=True),
        lax.psum_scatter(out_grad, ("rows", "seq"), scatter_dimension=0, tiled=True),
        lax.psum_scatter(gain_two_grad, ("rows", "seq"), scatter_dimension=0, tiled=True),
        lax.psum_scatter(up_grad, ("rows", "seq"), scatter_dimension=0, tiled=True),
        lax.psum_scatter(bias_up_grad, ("rows", "seq"), scatter_dimension=0, tiled=True),
        lax.psum_scatter(down_grad, ("rows", "seq"), scatter_dimension=0, tiled=True),
        lax.psum_scatter(bias_down_grad, ("rows", "seq"), scatter_dimension=0, tiled=True),
    )
    return (
        output,
        input_grad,
        skip_grad,
        skip_share,
        gain_one_share,
        qkv_share,
        out_share,
        gain_two_share,
        up_share,
        bias_up_share,
        down_share,
        bias_down_share,
    )


def solution(mesh):
    return jax.shard_map(
        body,
        mesh=mesh,
        in_specs=(
            P("rows", "seq", None),
            P("rows", "seq", None),
            P("rows", None),
            P("rows", None),
            P(),
            P(),
            P(),
            P(),
            P(),
            P(),
            P(),
            P(),
            P(),
            P("rows", "seq", None),
        ),
        out_specs=(
            P("rows", "seq", None),
            P("rows", "seq", None),
            P("rows", "seq", None),
            P(("rows", "seq"), None),
            P(("rows", "seq")),
            P(("rows", "seq"), None),
            P(("rows", "seq"), None),
            P(("rows", "seq")),
            P(("rows", "seq"), None),
            P(("rows", "seq")),
            P(("rows", "seq"), None),
            P(("rows", "seq")),
        ),
        check_vma=False,
    )
```

profile of v0, /device:TPU:3, one launch (start us, length us, event | category | flops | bytes accessed | tf_op | source)
XLA Modules:
  0.0 1326.1 jit_solution(4575809649064550022)
XLA Ops:
  37.1 35.0 %all-to-all-done = bf16[1,512,3,4,256]{4,1,2,0,3:T(8,128)(2,1)} async-done(((bf16[1,512,3,4,256]{4,1,2,0,3:T(8,128)(2,1)}), bf16[1,512,3,4,256]{4,1,2,0,3:T(8,128)(2,1)}, u32[]{:S(2)}, u32[]{:S(2)}) %all-to-all-start) | async-done | bytes 3145760 | tf_op jit(solution)/shard_map/all_to_all | solution.py:183
  91.1 90.9 %while.46 = (s32[]{:T(128)}, bf16[4,512,4,64]{1,3,2,0:T(8,128)(2,1)}, f32[4,4,512]{2,1,0:T(4,128)S(1)}, s32[4,512]{1,0:T(4,128)S(1)}, s32[2048]{0:T(1024)S(1)}, ...) while((s32[]{:T(128)}, ...), condition=%wide.region_5.6_spmd.clone, body=%wide.region_2.5_spmd.clone.sunk | while | flops 1152516096 | bytes 99192080 | solution.py:75
  194.8 11.8 reduce.26
  212.7 13.6 %all-to-all-done.1 = bf16[4,2,65536]{2,1,0:T(2,128)(2,1)S(1)} async-done(((bf16[4,2,65536]{2,1,0:T(2,128)(2,1)}), bf16[4,2,65536]{2,1,0:T(2,128)(2,1)S(1)}, u32[]{:S(2)}, u32[]{:S(2)}) %all-to-all-start.1) | async-done | bytes 1048608 | tf_op jit(solution)/shard_map/all_to_all | solution.py:191
  236.2 27.8 %multiply_convert_fusion.1 = (bf16[512,4096]{1,0:T(8,128)(2,1)}, f32[512,4096]{1,0:T(8,128)}, f32[512,4096]{1,0:T(8,128)}) fusion(f32[4096]{0:T(1024)S(1)} %convert_element_type.104, bf16[1024,4096]{1,0:T(8,128)(2,1)} %param.27, f32[512,1024]{1,0:T(8,128)S(1)} %get-tuple-element.449, f32[1024]{0:T(1024)S(1)} %convert_element_type.102, ...), kind=kOutput, calls=%fused_computation.65 | convolution fusion | flops 4435476480 | bytes 31481856 | tf_op jit(solution)/shard_map/rfd,dk->rfk/dot_general | solution.py:198
  264.0 14.0 %convert_reduce_fusion = (f32[4096]{0:T(1024)}, bf16[512,4096]{1,0:T(8,128)(2,1)S(1)}) fusion(f32[512,4096]{1,0:T(8,128)} %get-tuple-element.430, bf16[4096,1024]{1,0:T(8,128)(2,1)} %param.29, bf16[1,512,1024]{2,1,0:T(8,128)(2,1)S(1)} %copy-done.18, f32[512,4096]{1,0:T(8,128)} %get-tuple-element.450, f32[4096]{0:T(1024)S(1)} %convert_element_type.104), kind=kOutput, calls=%fused_computation.63 | convolution fusion | flops 4330614784 | bytes 30441472 | tf_op jit(solution)/shard_map/rfd,kd->rfk/dot_general | solution.py:210
  278.0 9.6 multiply_reduce_fusion.1
  306.2 11.3 all-to-all-done.2
  319.7 236.1 %while.47 = (s32[]{:T(128)}, f32[2048,4,64]{0,2,1:T(8,128)}, f32[2048,4,64]{0,2,1:T(8,128)}, bf16[4,512,4,64]{1,3,2,0:T(8,128)(2,1)}, bf16[4,512,4,64]{1,3,2,0:T...) while((s32[]{:T(128)}, f32[2048,4,64]{0,2,1:T(8,128)}, ...), condition=%wide.region_12.13_spmd.clone, body=%wide.region_10.12_spmd.clone.sunk | while | flops 2740584448 | bytes 224997680 | solution.py:131
  321.2 9.1 fusion.136
  331.1 14.0 %multiply_reduce_fusion.10 = (f32[4,512]{1,0:T(4,128)S(1)}, f32[4,512,2048]{2,1,0:T(8,128)}) fusion(f32[4,512,2048]{2,1,0:T(8,128)} %fusion.136, f32[4,512]{1,0:T(4,128)S(1)} %dynamic-slice_bitcast_fusion.2, f32[512,2048]{1,0:T(8,128)S(1)} %abs_convert_fusion.5, f32[4]{0:T(128)S(1)} %multiply_exponential_fusion.5, ...), kind=kOutput, calls=%fused_computation.27.clone.1 | convolution fusion | flops 566228992 | bytes 40124944 | tf_op jit(solution)/shard_map/while/body/eval_jaxpr/while/body/eval_jaxpr/qhd,khd->hqk/dot_general | solution.py:39
  345.1 15.2 %multiply_convert_fusion.9 = bf16[4,512,2048]{2,1,0:T(8,128)(2,1)} fusion(f32[4,512,2048]{2,1,0:T(8,128)} %get-tuple-element.627, f32[4,512,2048]{2,1,0:T(8,128)} %fusion.136, f32[4,512]{1,0:T(4,128)S(1)} %get-tuple-element.628), kind=kLoop, calls=%fused_computation.26.clone.1 | loop fusion | flops 12582912 | bytes 41951232 | tf_op jit(solution)/shard_map/while/body/eval_jaxpr/while/body/eval_jaxpr/convert_element_type | solution.py:118
  379.3 9.1 fusion.136
  389.1 14.0 %multiply_reduce_fusion.10 = (f32[4,512]{1,0:T(4,128)S(1)}, f32[4,512,2048]{2,1,0:T(8,128)}) fusion(f32[4,512,2048]{2,1,0:T(8,128)} %fusion.136, f32[4,512]{1,0:T(4,128)S(1)} %dynamic-slice_bitcast_fusion.2, f32[512,2048]{1,0:T(8,128)S(1)} %abs_convert_fusion.5, f32[4]{0:T(128)S(1)} %multiply_exponential_fusion.5, ...), kind=kOutput, calls=%fused_computation.27.clone.1 | convolution fusion | flops 566228992 | bytes 40124944 | tf_op jit(solution)/shard_map/while/body/eval_jaxpr/while/body/eval_jaxpr/qhd,khd->hqk/dot_general | solution.py:39
  403.1 15.1 %multiply_convert_fusion.9 = bf16[4,512,2048]{2,1,0:T(8,128)(2,1)} fusion(f32[4,512,2048]{2,1,0:T(8,128)} %get-tuple-element.627, f32[4,512,2048]{2,1,0:T(8,128)} %fusion.136, f32[4,512]{1,0:T(4,128)S(1)} %get-tuple-element.628), kind=kLoop, calls=%fused_computation.26.clone.1 | loop fusion | flops 12582912 | bytes 41951232 | tf_op jit(solution)/shard_map/while/body/eval_jaxpr/while/body/eval_jaxpr/convert_element_type | solution.py:118
  438.7 9.1 fusion.136
  448.6 13.9 %multiply_reduce_fusion.10 = (f32[4,512]{1,0:T(4,128)S(1)}, f32[4,512,2048]{2,1,0:T(8,128)}) fusion(f32[4,512,2048]{2,1,0:T(8,128)} %fusion.136, f32[4,512]{1,0:T(4,128)S(1)} %dynamic-slice_bitcast_fusion.2, f32[512,2048]{1,0:T(8,128)S(1)} %abs_convert_fusion.5, f32[4]{0:T(128)S(1)} %multiply_exponential_fusion.5, ...), kind=kOutput, calls=%fused_computation.27.clone.1 | convolution fusion | flops 566228992 | bytes 40124944 | tf_op jit(solution)/shard_map/while/body/eval_jaxpr/while/body/eval_jaxpr/qhd,khd->hqk/dot_general | solution.py:39
  462.5 15.0 %multiply_convert_fusion.9 = bf16[4,512,2048]{2,1,0:T(8,128)(2,1)} fusion(f32[4,512,2048]{2,1,0:T(8,128)} %get-tuple-element.627, f32[4,512,2048]{2,1,0:T(8,128)} %fusion.136, f32[4,512]{1,0:T(4,128)S(1)} %get-tuple-element.628), kind=kLoop, calls=%fused_computation.26.clone.1 | loop fusion | flops 12582912 | bytes 41951232 | tf_op jit(solution)/shard_map/while/body/eval_jaxpr/while/body/eval_jaxpr/convert_element_type | solution.py:118
  497.9 9.1 fusion.136
  507.8 13.9 %multiply_reduce_fusion.10 = (f32[4,512]{1,0:T(4,128)S(1)}, f32[4,512,2048]{2,1,0:T(8,128)}) fusion(f32[4,512,2048]{2,1,0:T(8,128)} %fusion.136, f32[4,512]{1,0:T(4,128)S(1)} %dynamic-slice_bitcast_fusion.2, f32[512,2048]{1,0:T(8,128)S(1)} %abs_convert_fusion.5, f32[4]{0:T(128)S(1)} %multiply_exponential_fusion.5, ...), kind=kOutput, calls=%fused_computation.27.clone.1 | convolution fusion | flops 566228992 | bytes 40124944 | tf_op jit(solution)/shard_map/while/body/eval_jaxpr/while/body/eval_jaxpr/qhd,khd->hqk/dot_general | solution.py:39
  521.7 15.0 %multiply_convert_fusion.9 = bf16[4,512,2048]{2,1,0:T(8,128)(2,1)} fusion(f32[4,512,2048]{2,1,0:T(8,128)} %get-tuple-element.627, f32[4,512,2048]{2,1,0:T(8,128)} %fusion.136, f32[4,512]{1,0:T(4,128)S(1)} %get-tuple-element.628), kind=kLoop, calls=%fused_computation.26.clone.1 | loop fusion | flops 12582912 | bytes 41951232 | tf_op jit(solution)/shard_map/while/body/eval_jaxpr/while/body/eval_jaxpr/convert_element_type | solution.py:118
  570.8 52.3 %all_to_all.60 = bf16[1,2048,3,1,256]{4,2,3,0,1:T(4,128)(2,1)S(1)} all-to-all(bf16[1,2048,3,1,256]{4,2,3,0,1:T(4,128)(2,1)} %copy.73), channel_id=1, replica_groups=mesh['rows'=8,'seq'=4] {'seq'}, dimensions={1} | all-to-all | bytes 6291456 | tf_op jit(solution)/shard_map/all_to_all | solution.py:244
  630.0 8.6 fusion.69
  638.7 8.6 multiply_reduce_fusion.2
  656.5 11.3 fusion.70
  669.1 11.1 fusion.59
  680.9 10.8 fusion.52
  691.8 43.6 %all-reduce.4 = (f32[1024]{0:T(1024)S(1)}, f32[1024]{0:T(1024)S(1)}, f32[4096]{0:T(1024)S(1)}, f32[1024]{0:T(1024)S(1)}) all-reduce(f32[1024]{0:T(1024)S(1)} %get-tuple-element.369, f32[1024]{0:T(1024)S(1)} %copy-done.41, f32[4096]{0:T(1024)S(1)} %copy-done.35, ...), channel_id=3, replica_groups=mesh['rows'=8,'seq'=4] {'rows','seq'}, use_global_device_ids=true, to_apply=%region_17.18.clone | all-reduce | flops 7168 | bytes 57344
  743.9 50.7 %reduce-scatter.8.cloned.1.call-done = f32[32,3072]{1,0:T(8,128)} async-done(((f32[1024,3072]{1,0:T(8,128)}), f32[32,3072]{1,0:T(8,128)}) %reduce-scatter.8.cloned.1.call-update) | async-done | bytes 393232 | tf_op jit(solution)/shard_map/reduce_scatter | solution.py:267
  794.7 139.3 %reduce-scatter.6.cloned.1.call-done = f32[64,1024]{1,0:T(8,128)} async-done(((f32[2048,1024]{1,0:T(8,128)}), f32[64,1024]{1,0:T(8,128)}) %reduce-scatter.6.cloned.1.call-update) | async-done | bytes 262160 | tf_op jit(solution)/shard_map/reduce_scatter | solution.py:265
  934.0 197.1 %reduce-scatter.12.cloned.1.call-done = f32[32,4096]{1,0:T(8,128)} async-done(((f32[1024,4096]{1,0:T(8,128)}), f32[32,4096]{1,0:T(8,128)}) %reduce-scatter.12.cloned.1.call-update) | async-done | bytes 524304 | tf_op jit(solution)/shard_map/reduce_scatter | solution.py:270
  1131.1 188.2 %reduce-scatter.14.cloned.1.call-done = f32[128,1024]{1,0:T(8,128)} async-done(((f32[4096,1024]{1,0:T(8,128)}), f32[128,1024]{1,0:T(8,128)}) %reduce-scatter.14.cloned.1.call-update) | async-done | bytes 524304 | tf_op jit(solution)/shard_map/reduce_scatter | solution.py:272
  (281 shorter events, 313.5 us)
Async XLA Ops:
  7.2 225.6 %copy-start = (bf16[1024,1024]{1,0:T(8,128)(2,1)S(1)}, bf16[1024,1024]{1,0:T(8,128)(2,1)}, u32[]{:S(2)}) copy-start(bf16[1024,1024]{1,0:T(8,128)(2,1)} %param.25) | copy-start | bytes 6291460
  30.5 41.6 %all-to-all-start = ((bf16[1,512,3,4,256]{4,1,2,0,3:T(8,128)(2,1)}), bf16[1,512,3,4,256]{4,1,2,0,3:T(8,128)(2,1)}, u32[]{:S(2)}, u32[]{:S(2)}) async-start(bf16[1,512,3,4,256]{4,1,2,0,3:T(8,128)(2,1)} %copy.63), calls=%async_computation | async-start | bytes 6291456 | tf_op jit(solution)/shard_map/all_to_all | solution.py:183
  194.3 18.3 %copy-start.43 = (bf16[1024]{0:T(1024)(128)(2,1)S(1)}, bf16[1024]{0:T(1024)(128)(2,1)}, u32[]{:S(2)}) copy-start(bf16[1024]{0:T(1024)(128)(2,1)} %param.26) | copy-start | bytes 6148
  194.3 18.3 %copy-start.38 = (bf16[4096]{0:T(1024)(128)(2,1)S(1)}, bf16[4096]{0:T(1024)(128)(2,1)}, u32[]{:S(2)}) copy-start(bf16[4096]{0:T(1024)(128)(2,1)} %param.28) | copy-start | bytes 24580
  208.3 17.9 %all-to-all-start.1 = ((bf16[4,2,65536]{2,1,0:T(2,128)(2,1)}), bf16[4,2,65536]{2,1,0:T(2,128)(2,1)S(1)}, u32[]{:S(2)}, u32[]{:S(2)}) async-start(bf16[4,2,65536]{2,1,0:T(2,128)(2,1)} %reshape.628), calls=%async_computation.1 | async-start | bytes 2097152 | tf_op jit(solution)/shard_map/all_to_all | solution.py:191
  212.7 74.9 %copy-start.31 = (f32[1024]{0:T(1024)}, f32[1024]{0:T(1024)S(1)}, u32[]{:S(2)}) copy-start(f32[1024]{0:T(1024)S(1)} %convert_element_type.102) | copy-start | bytes 12292
  235.8 51.8 %copy-start.12 = (f32[512,1024]{1,0:T(8,128)}, f32[512,1024]{1,0:T(8,128)S(1)}, u32[]{:S(2)}) copy-start(f32[512,1024]{1,0:T(8,128)S(1)} %get-tuple-element.449) | copy-start | bytes 6291460
  235.8 51.8 %copy-start.26 = (f32[512]{0:T(512)}, f32[512]{0:T(512)S(1)}, u32[]{:S(2)}) copy-start(f32[512]{0:T(512)S(1)} %broadcast_multiply_fusion.4) | copy-start | bytes 6148
  236.1 51.4 %copy-start.36 = (f32[512]{0:T(512)}, f32[512]{0:T(512)S(1)}, u32[]{:S(2)}) copy-start(f32[512]{0:T(512)S(1)} %add_rsqrt_fusion) | copy-start | bytes 6148
  236.1 27.8 %copy-start.18 = (bf16[1,512,1024]{2,1,0:T(8,128)(2,1)S(1)}, bf16[1,512,1024]{2,1,0:T(8,128)(2,1)}, u32[]{:S(2)}) copy-start(bf16[1,512,1024]{2,1,0:T(8,128)(2,1)} %param.31) | copy-start | bytes 3145732
  292.6 10.2 copy-start.10
  297.8 19.7 %all-to-all-start.2 = ((bf16[1,512,4,256]{3,1,0,2:T(8,128)(2,1)}), bf16[1,512,4,256]{3,1,0,2:T(8,128)(2,1)}, u32[]{:S(2)}, u32[]{:S(2)}) async-start(bf16[1,512,4,256]{3,1,0,2:T(8,128)(2,1)} %copy.69), calls=%async_computation.2 | async-start | bytes 2097152 | tf_op jit(solution)/shard_map/all_to_all | solution.py:222
  302.9 441.1 %reduce-scatter.10.cloned.1.call-start = ((), (), s32[]{:S(2)}) async-start(), calls=%async_computation.11 | async-start | bytes 4325376 | tf_op jit(solution)/shard_map/reduce_scatter | solution.py:268
  306.1 13.6 %copy-start.5 = (bf16[2048,4,64]{0,2,1:T(8,128)(2,1)S(1)}, bf16[2048,4,64]{0,2,1:T(8,128)(2,1)}, u32[]{:S(2)}) copy-start(bf16[2048,4,64]{0,2,1:T(8,128)(2,1)} %get-tuple-element.718) | copy-start | bytes 3145732
  306.1 13.6 %copy-start.8 = (bf16[2048,4,64]{0,2,1:T(8,128)(2,1)S(1)}, bf16[2048,4,64]{0,2,1:T(8,128)(2,1)}, u32[]{:S(2)}) copy-start(bf16[2048,4,64]{0,2,1:T(8,128)(2,1)} %get-tuple-element.719) | copy-start | bytes 3145732
  306.1 488.5 %reduce-scatter.8.cloned.1.call-start = ((), (), s32[]{:S(2)}) async-start(), calls=%async_computation.10 | async-start | bytes 12976128 | tf_op jit(solution)/shard_map/reduce_scatter | solution.py:267
  345.1 21.8 %copy-start.20 = (bf16[4,512,4,64]{1,3,2,0:T(8,128)(2,1)S(1)}, bf16[4,512,4,64]{1,3,2,0:T(8,128)(2,1)}, u32[]{:S(2)}) copy-start(bf16[4,512,4,64]{1,3,2,0:T(8,128)(2,1)} %get-tuple-element.684) | copy-start | bytes 3145732 | tf_op jit(solution)/shard_map/while/body/eval_jaxpr/while
  360.2 13.4 %copy-start.2 = (f32[4,512,2048]{2,1,0:T(8,128)S(1)}, f32[4,512,2048]{2,1,0:T(8,128)}, u32[]{:S(2)}) copy-start(f32[4,512,2048]{2,1,0:T(8,128)} %get-tuple-element.627) | copy-start | bytes 50331652 | tf_op jit(solution)/shard_map/while/body/eval_jaxpr/while
  403.1 22.3 %copy-start.20 = (bf16[4,512,4,64]{1,3,2,0:T(8,128)(2,1)S(1)}, bf16[4,512,4,64]{1,3,2,0:T(8,128)(2,1)}, u32[]{:S(2)}) copy-start(bf16[4,512,4,64]{1,3,2,0:T(8,128)(2,1)} %get-tuple-element.684) | copy-start | bytes 3145732 | tf_op jit(solution)/shard_map/while/body/eval_jaxpr/while
  418.2 14.0 %copy-start.2 = (f32[4,512,2048]{2,1,0:T(8,128)S(1)}, f32[4,512,2048]{2,1,0:T(8,128)}, u32[]{:S(2)}) copy-start(f32[4,512,2048]{2,1,0:T(8,128)} %get-tuple-element.627) | copy-start | bytes 50331652 | tf_op jit(solution)/shard_map/while/body/eval_jaxpr/while
  462.5 22.2 %copy-start.20 = (bf16[4,512,4,64]{1,3,2,0:T(8,128)(2,1)S(1)}, bf16[4,512,4,64]{1,3,2,0:T(8,128)(2,1)}, u32[]{:S(2)}) copy-start(bf16[4,512,4,64]{1,3,2,0:T(8,128)(2,1)} %get-tuple-element.684) | copy-start | bytes 3145732 | tf_op jit(solution)/shard_map/while/body/eval_jaxpr/while
  477.5 14.0 %copy-start.2 = (f32[4,512,2048]{2,1,0:T(8,128)S(1)}, f32[4,512,2048]{2,1,0:T(8,128)}, u32[]{:S(2)}) copy-start(f32[4,512,2048]{2,1,0:T(8,128)} %get-tuple-element.627) | copy-start | bytes 50331652 | tf_op jit(solution)/shard_map/while/body/eval_jaxpr/while
  521.7 22.2 %copy-start.20 = (bf16[4,512,4,64]{1,3,2,0:T(8,128)(2,1)S(1)}, bf16[4,512,4,64]{1,3,2,0:T(8,128)(2,1)}, u32[]{:S(2)}) copy-start(bf16[4,512,4,64]{1,3,2,0:T(8,128)(2,1)} %get-tuple-element.684) | copy-start | bytes 3145732 | tf_op jit(solution)/shard_map/while/body/eval_jaxpr/while
  536.7 14.0 %copy-start.2 = (f32[4,512,2048]{2,1,0:T(8,128)S(1)}, f32[4,512,2048]{2,1,0:T(8,128)}, u32[]{:S(2)}) copy-start(f32[4,512,2048]{2,1,0:T(8,128)} %get-tuple-element.627) | copy-start | bytes 50331652 | tf_op jit(solution)/shard_map/while/body/eval_jaxpr/while
  638.7 295.3 %reduce-scatter.6.cloned.1.call-start = ((), (), s32[]{:S(2)}) async-start(), calls=%async_computation.9 | async-start | bytes 8650752 | tf_op jit(solution)/shard_map/reduce_scatter | solution.py:265
  654.8 476.3 %reduce-scatter.12.cloned.1.call-start = ((), (), s32[]{:S(2)}) async-start(), calls=%async_computation.12 | async-start | bytes 17301504 | tf_op jit(solution)/shard_map/reduce_scatter | solution.py:270
  667.8 651.5 %reduce-scatter.14.cloned.1.call-start = ((), (), s32[]{:S(2)}) async-start(), calls=%async_computation.13 | async-start | bytes 17301504 | tf_op jit(solution)/shard_map/reduce_scatter | solution.py:272
  680.9 10.9 copy-start.30
  680.9 10.9 copy-start.35
  680.9 10.9 copy-start.41
  680.9 56.8 %copy-start.23 = (bf16[512,1024]{1,0:T(8,128)(2,1)S(1)}, bf16[512,1024]{1,0:T(8,128)(2,1)}, u32[]{:S(2)}) copy-start(bf16[512,1024]{1,0:T(8,128)(2,1)} %copy-done.22) | copy-start | bytes 3145732
  737.7 581.6 %copy-start.1 = (bf16[1024,1024]{1,0:T(8,128)(2,1)S(1)}, bf16[1024,1024]{1,0:T(8,128)(2,1)}, u32[]{:S(2)}) copy-start(bf16[1024,1024]{1,0:T(8,128)(2,1)} %param.25) | copy-start | bytes 6291460
  (43 other events, 179.0 us)
Sparse Core Ops, SparseCore 0:
  306.5 126.9 reduce-scatter.9
  638.8 155.8 reduce-scatter.7
  797.6 136.2 reduce-scatter.5
  936.8 194.2 reduce-scatter.11
  1133.9 185.3 reduce-scatter.13
where the time goes:
time: 1330 us
  waiting for transfers between devices  635 us (48%)
  matrix products  355 us (27%)
  other arithmetic  121 us (9%)
  blocking collectives  95.9 us (7%)
  local copies, waits for them, and re-layouts  87.9 us (7%)
  starting transfers between devices  15.2 us (1%)
  between operations  14.4 us (1%)
    reduce_scatter x1, waiting for transfers between devices, body(): lax.psum_scatter(up_grad, ('rows', 'seq'), scatter_dimension=0, tiled=True)  197 us
    reduce_scatter x1, waiting for transfers between devices, body(): lax.psum_scatter(down_grad, ('rows', 'seq'), scatter_dimension=0, tiled=T...  188 us
    reduce_scatter x1, waiting for transfers between devices, body(): lax.psum_scatter(skip_w_grad, ('rows', 'seq'), scatter_dimension=0, tiled...  139 us
    dot_general x8, matrix products, block_scores(): jnp.einsum('qhd,khd->hqk', q_blk, all_keys, preferred_element_type=jnp.fl...  80.9 us
    convert_element_type x4, other arithmetic, one_block(): score_grad = (soft * (prob_grad - jnp.sum(soft * prob_grad, axis=-1, keep...  60.2 us
    all_to_all x1, blocking collectives, body(): lax.all_to_all(packed_grad, 'seq', split_axis=1, concat_axis=3, tiled=True)  52.3 us
    reduce_scatter x1, waiting for transfers between devices, body(): lax.psum_scatter(qkv_grad, ('rows', 'seq'), scatter_dimension=0, tiled=True)  50.7 us
    unnamed x1, blocking collectives  43.6 us
  transfers between devices with their start and end apart: 8, of which 7 were waited for; matrix products, arithmetic and copies ran while one was open for 25% of the time, Pallas kernels for 0%

commit v1 on v0

--- a/solution.py
+++ b/solution.py
@@ -241,7 +241,12 @@
         )
 
     packed_grad = lax.map(backward_row, (by_heads, log_total, grad_heads, seg_ids, frame_valid))
-    packed_back = lax.all_to_all(packed_grad, "seq", split_axis=1, concat_axis=3, tiled=True)
+    packed_back = jnp.concatenate(
+        lax.all_to_all(
+            jnp.stack(jnp.split(packed_grad, lax.axis_size("seq"), axis=1)), "seq", 0, 0
+        ),
+        axis=3,
+    )
     packed_back = packed_back.reshape(rows_here, frames, 3 * D)
     qkv_grad = jnp.einsum("rfd,rfe->de", normed, packed_back, preferred_element_type=jnp.float32)
     normed_grad = jnp.einsum("rfe,de->rfd", packed_back, w_qkv, preferred_element_type=jnp.float32)

time: 1330 us -> 1310 us (0.985)
  transfers between devices with their start and end apart: 8 -> 8, of which waited for: 7 -> 7; matrix products, arithmetic and copies ran while one was open for 25% -> 24% of each run, Pallas kernels for 0% -> 0%
where the time goes in v1:
time: 1310 us; the launch traced here: 1300 us
  waiting for transfers between devices  634 us (48%)
  matrix products  354 us (27%)
  other arithmetic  120 us (9%)
  blocking collectives  83.3 us (6%)
  local copies, waits for them, and re-layouts  77.9 us (6%)
  starting transfers between devices  15 us (1%)
  between operations  14.5 us (1%)
    reduce_scatter x1, waiting for transfers between devices, body(): lax.psum_scatter(up_grad, ('rows', 'seq'), scatter_dimension=0, tiled=True)  199 us
    reduce_scatter x1, waiting for transfers between devices, body(): lax.psum_scatter(down_grad, ('rows', 'seq'), scatter_dimension=0, tiled=T...  187 us
    reduce_scatter x1, waiting for transfers between devices, body(): lax.psum_scatter(skip_w_grad, ('rows', 'seq'), scatter_dimension=0, tiled...  138 us
    dot_general x8, matrix products, block_scores(): jnp.einsum('qhd,khd->hqk', q_blk, all_keys, preferred_element_type=jnp.fl...  80.8 us
    convert_element_type x4, other arithmetic, one_block(): score_grad = (soft * (prob_grad - jnp.sum(soft * prob_grad, axis=-1, keep...  60.2 us
    reduce_scatter x1, waiting for transfers between devices, body(): lax.psum_scatter(qkv_grad, ('rows', 'seq'), scatter_dimension=0, tiled=True)  50.7 us
    unnamed x1, blocking collectives  43.5 us
    all_to_all x1, blocking collectives, body(): lax.all_to_all(jnp.stack(jnp.split(packed_grad, lax.axis_size('seq'), axi...  39.8 us
  transfers between devices with their start and end apart: 8, of which 7 were waited for; matrix products, arithmetic and copies ran while one was open for 24% of the time, Pallas kernels for 0%

profile of v1, /device:TPU:3, one launch (start us, length us, event | category | flops | bytes accessed | tf_op | source)
XLA Modules:
  0.0 1299.4 jit_solution(10385991138284285976)
XLA Ops:
  37.1 35.0 %all-to-all-done = bf16[1,512,3,4,256]{4,1,2,0,3:T(8,128)(2,1)} async-done(((bf16[1,512,3,4,256]{4,1,2,0,3:T(8,128)(2,1)}), bf16[1,512,3,4,256]{4,1,2,0,3:T(8,128)(2,1)}, u32[]{:S(2)}, u32[]{:S(2)}) %all-to-all-start) | async-done | bytes 3145760 | tf_op jit(solution)/shard_map/all_to_all | solution.py:183
  91.1 90.9 %while.46 = (s32[]{:T(128)}, bf16[4,512,4,64]{1,3,2,0:T(8,128)(2,1)}, f32[4,4,512]{2,1,0:T(4,128)S(1)}, s32[4,512]{1,0:T(4,128)S(1)}, s32[2048]{0:T(1024)S(1)}, ...) while((s32[]{:T(128)}, ...), condition=%wide.region_5.6_spmd.clone, body=%wide.region_2.5_spmd.clone.sunk | while | flops 1152516096 | bytes 99192080 | solution.py:75
  186.0 8.2 reshape.617
  194.7 11.8 reduce.26
  212.6 13.6 %all-to-all-done.1 = bf16[4,2,65536]{2,1,0:T(2,128)(2,1)S(1)} async-done(((bf16[4,2,65536]{2,1,0:T(2,128)(2,1)}), bf16[4,2,65536]{2,1,0:T(2,128)(2,1)S(1)}, u32[]{:S(2)}, u32[]{:S(2)}) %all-to-all-start.1) | async-done | bytes 1048608 | tf_op jit(solution)/shard_map/all_to_all | solution.py:191
  236.1 27.8 %multiply_convert_fusion.1 = (bf16[512,4096]{1,0:T(8,128)(2,1)}, f32[512,4096]{1,0:T(8,128)}, f32[512,4096]{1,0:T(8,128)}) fusion(f32[4096]{0:T(1024)S(1)} %convert_element_type.104, bf16[1024,4096]{1,0:T(8,128)(2,1)} %param.27, f32[512,1024]{1,0:T(8,128)S(1)} %get-tuple-element.454, f32[1024]{0:T(1024)S(1)} %convert_element_type.102, ...), kind=kOutput, calls=%fused_computation.65 | convolution fusion | flops 4435476480 | bytes 31481856 | tf_op jit(solution)/shard_map/rfd,dk->rfk/dot_general | solution.py:198
  263.9 14.0 %convert_reduce_fusion = (f32[4096]{0:T(1024)}, bf16[512,4096]{1,0:T(8,128)(2,1)S(1)}) fusion(f32[512,4096]{1,0:T(8,128)} %get-tuple-element.430, bf16[4096,1024]{1,0:T(8,128)(2,1)} %param.29, bf16[1,512,1024]{2,1,0:T(8,128)(2,1)S(1)} %copy-done.18, f32[512,4096]{1,0:T(8,128)} %get-tuple-element.455, f32[4096]{0:T(1024)S(1)} %convert_element_type.104), kind=kOutput, calls=%fused_computation.63 | convolution fusion | flops 4330614784 | bytes 30441472 | tf_op jit(solution)/shard_map/rfd,kd->rfk/dot_general | solution.py:210
  277.9 9.5 multiply_reduce_fusion.1
  306.0 11.3 all-to-all-done.2
  319.6 235.9 %while.47 = (s32[]{:T(128)}, f32[2048,4,64]{0,2,1:T(8,128)}, f32[2048,4,64]{0,2,1:T(8,128)}, bf16[4,512,4,64]{1,3,2,0:T(8,128)(2,1)}, bf16[4,512,4,64]{1,3,2,0:T...) while((s32[]{:T(128)}, f32[2048,4,64]{0,2,1:T(8,128)}, ...), condition=%wide.region_12.13_spmd.clone, body=%wide.region_10.12_spmd.clone.sunk | while | flops 2740584448 | bytes 224997680 | solution.py:131
  321.1 9.1 fusion.137
  330.9 14.0 %multiply_reduce_fusion.10 = (f32[4,512]{1,0:T(4,128)S(1)}, f32[4,512,2048]{2,1,0:T(8,128)}) fusion(f32[4,512,2048]{2,1,0:T(8,128)} %fusion.137, f32[4,512]{1,0:T(4,128)S(1)} %dynamic-slice_bitcast_fusion.2, f32[512,2048]{1,0:T(8,128)S(1)} %abs_convert_fusion.5, f32[4]{0:T(128)S(1)} %multiply_exponential_fusion.5, ...), kind=kOutput, calls=%fused_computation.27.clone.1 | convolution fusion | flops 566228992 | bytes 40124944 | tf_op jit(solution)/shard_map/while/body/eval_jaxpr/while/body/eval_jaxpr/qhd,khd->hqk/dot_general | solution.py:39
  344.9 15.2 %multiply_convert_fusion.9 = bf16[4,512,2048]{2,1,0:T(8,128)(2,1)} fusion(f32[4,512,2048]{2,1,0:T(8,128)} %get-tuple-element.632, f32[4,512,2048]{2,1,0:T(8,128)} %fusion.137, f32[4,512]{1,0:T(4,128)S(1)} %get-tuple-element.633), kind=kLoop, calls=%fused_computation.26.clone.1 | loop fusion | flops 12582912 | bytes 41951232 | tf_op jit(solution)/shard_map/while/body/eval_jaxpr/while/body/eval_jaxpr/convert_element_type | solution.py:118
  379.1 9.1 fusion.137
  388.9 14.0 %multiply_reduce_fusion.10 = (f32[4,512]{1,0:T(4,128)S(1)}, f32[4,512,2048]{2,1,0:T(8,128)}) fusion(f32[4,512,2048]{2,1,0:T(8,128)} %fusion.137, f32[4,512]{1,0:T(4,128)S(1)} %dynamic-slice_bitcast_fusion.2, f32[512,2048]{1,0:T(8,128)S(1)} %abs_convert_fusion.5, f32[4]{0:T(128)S(1)} %multiply_exponential_fusion.5, ...), kind=kOutput, calls=%fused_computation.27.clone.1 | convolution fusion | flops 566228992 | bytes 40124944 | tf_op jit(solution)/shard_map/while/body/eval_jaxpr/while/body/eval_jaxpr/qhd,khd->hqk/dot_general | solution.py:39
  402.9 15.1 %multiply_convert_fusion.9 = bf16[4,512,2048]{2,1,0:T(8,128)(2,1)} fusion(f32[4,512,2048]{2,1,0:T(8,128)} %get-tuple-element.632, f32[4,512,2048]{2,1,0:T(8,128)} %fusion.137, f32[4,512]{1,0:T(4,128)S(1)} %get-tuple-element.633), kind=kLoop, calls=%fused_computation.26.clone.1 | loop fusion | flops 12582912 | bytes 41951232 | tf_op jit(solution)/shard_map/while/body/eval_jaxpr/while/body/eval_jaxpr/convert_element_type | solution.py:118
  438.4 9.1 fusion.137
  448.3 13.9 %multiply_reduce_fusion.10 = (f32[4,512]{1,0:T(4,128)S(1)}, f32[4,512,2048]{2,1,0:T(8,128)}) fusion(f32[4,512,2048]{2,1,0:T(8,128)} %fusion.137, f32[4,512]{1,0:T(4,128)S(1)} %dynamic-slice_bitcast_fusion.2, f32[512,2048]{1,0:T(8,128)S(1)} %abs_convert_fusion.5, f32[4]{0:T(128)S(1)} %multiply_exponential_fusion.5, ...), kind=kOutput, calls=%fused_computation.27.clone.1 | convolution fusion | flops 566228992 | bytes 40124944 | tf_op jit(solution)/shard_map/while/body/eval_jaxpr/while/body/eval_jaxpr/qhd,khd->hqk/dot_general | solution.py:39
  462.2 15.0 %multiply_convert_fusion.9 = bf16[4,512,2048]{2,1,0:T(8,128)(2,1)} fusion(f32[4,512,2048]{2,1,0:T(8,128)} %get-tuple-element.632, f32[4,512,2048]{2,1,0:T(8,128)} %fusion.137, f32[4,512]{1,0:T(4,128)S(1)} %get-tuple-element.633), kind=kLoop, calls=%fused_computation.26.clone.1 | loop fusion | flops 12582912 | bytes 41951232 | tf_op jit(solution)/shard_map/while/body/eval_jaxpr/while/body/eval_jaxpr/convert_element_type | solution.py:118
  497.6 9.1 fusion.137
  507.5 13.9 %multiply_reduce_fusion.10 = (f32[4,512]{1,0:T(4,128)S(1)}, f32[4,512,2048]{2,1,0:T(8,128)}) fusion(f32[4,512,2048]{2,1,0:T(8,128)} %fusion.137, f32[4,512]{1,0:T(4,128)S(1)} %dynamic-slice_bitcast_fusion.2, f32[512,2048]{1,0:T(8,128)S(1)} %abs_convert_fusion.5, f32[4]{0:T(128)S(1)} %multiply_exponential_fusion.5, ...), kind=kOutput, calls=%fused_computation.27.clone.1 | convolution fusion | flops 566228992 | bytes 40124944 | tf_op jit(solution)/shard_map/while/body/eval_jaxpr/while/body/eval_jaxpr/qhd,khd->hqk/dot_general | solution.py:39
  521.4 15.0 %multiply_convert_fusion.9 = bf16[4,512,2048]{2,1,0:T(8,128)(2,1)} fusion(f32[4,512,2048]{2,1,0:T(8,128)} %get-tuple-element.632, f32[4,512,2048]{2,1,0:T(8,128)} %fusion.137, f32[4,512]{1,0:T(4,128)S(1)} %get-tuple-element.633), kind=kLoop, calls=%fused_computation.26.clone.1 | loop fusion | flops 12582912 | bytes 41951232 | tf_op jit(solution)/shard_map/while/body/eval_jaxpr/while/body/eval_jaxpr/convert_element_type | solution.py:118
  563.6 39.8 %all_to_all.50 = bf16[4,1,512,3,1,256]{2,5,3,4,1,0:T(8,128)(2,1)S(1)} all-to-all(bf16[4,1,512,3,1,256]{2,5,3,4,1,0:T(8,128)(2,1)S(1)} %pad_maximum_fusion.1), channel_id=1, replica_groups=mesh['rows'=8,'seq'=4] {'seq'}, dimensions={0} | all-to-all | bytes 6291456 | tf_op jit(solution)/shard_map/all_to_all | solution.py:245
  612.9 8.6 multiply_reduce_fusion.2
  630.7 11.5 fusion.70
  643.5 11.1 fusion.59
  655.3 10.8 fusion.52
  666.1 43.5 %all-reduce.4 = (f32[1024]{0:T(1024)S(1)}, f32[1024]{0:T(1024)S(1)}, f32[4096]{0:T(1024)S(1)}, f32[1024]{0:T(1024)S(1)}) all-reduce(f32[1024]{0:T(1024)S(1)} %get-tuple-element.369, f32[1024]{0:T(1024)S(1)} %copy-done.41, f32[4096]{0:T(1024)S(1)} %copy-done.35, ...), channel_id=3, replica_groups=mesh['rows'=8,'seq'=4] {'rows','seq'}, use_global_device_ids=true, to_apply=%region_17.18.clone | all-reduce | flops 7168 | bytes 57344
  718.1 50.7 %reduce-scatter.8.cloned.1.call-done = f32[32,3072]{1,0:T(8,128)} async-done(((f32[1024,3072]{1,0:T(8,128)}), f32[32,3072]{1,0:T(8,128)}) %reduce-scatter.8.cloned.1.call-update) | async-done | bytes 393232 | tf_op jit(solution)/shard_map/reduce_scatter | solution.py:272
  768.8 138.5 %reduce-scatter.6.cloned.1.call-done = f32[64,1024]{1,0:T(8,128)} async-done(((f32[2048,1024]{1,0:T(8,128)}), f32[64,1024]{1,0:T(8,128)}) %reduce-scatter.6.cloned.1.call-update) | async-done | bytes 262160 | tf_op jit(solution)/shard_map/reduce_scatter | solution.py:270
  907.3 198.7 %reduce-scatter.12.cloned.1.call-done = f32[32,4096]{1,0:T(8,128)} async-done(((f32[1024,4096]{1,0:T(8,128)}), f32[32,4096]{1,0:T(8,128)}) %reduce-scatter.12.cloned.1.call-update) | async-done | bytes 524304 | tf_op jit(solution)/shard_map/reduce_scatter | solution.py:275
  1106.0 186.7 %reduce-scatter.14.cloned.1.call-done = f32[128,1024]{1,0:T(8,128)} async-done(((f32[4096,1024]{1,0:T(8,128)}), f32[128,1024]{1,0:T(8,128)}) %reduce-scatter.14.cloned.1.call-update) | async-done | bytes 524304 | tf_op jit(solution)/shard_map/reduce_scatter | solution.py:277
  (282 shorter events, 300.7 us)
Async XLA Ops:
  7.2 225.5 %copy-start = (bf16[1024,1024]{1,0:T(8,128)(2,1)S(1)}, bf16[1024,1024]{1,0:T(8,128)(2,1)}, u32[]{:S(2)}) copy-start(bf16[1024,1024]{1,0:T(8,128)(2,1)} %param.25) | copy-start | bytes 6291460
  30.5 41.6 %all-to-all-start = ((bf16[1,512,3,4,256]{4,1,2,0,3:T(8,128)(2,1)}), bf16[1,512,3,4,256]{4,1,2,0,3:T(8,128)(2,1)}, u32[]{:S(2)}, u32[]{:S(2)}) async-start(bf16[1,512,3,4,256]{4,1,2,0,3:T(8,128)(2,1)} %copy.73), calls=%async_computation | async-start | bytes 6291456 | tf_op jit(solution)/shard_map/all_to_all | solution.py:183
  194.2 18.3 %copy-start.43 = (bf16[1024]{0:T(1024)(128)(2,1)S(1)}, bf16[1024]{0:T(1024)(128)(2,1)}, u32[]{:S(2)}) copy-start(bf16[1024]{0:T(1024)(128)(2,1)} %param.26) | copy-start | bytes 6148
  194.2 18.3 %copy-start.38 = (bf16[4096]{0:T(1024)(128)(2,1)S(1)}, bf16[4096]{0:T(1024)(128)(2,1)}, u32[]{:S(2)}) copy-start(bf16[4096]{0:T(1024)(128)(2,1)} %param.28) | copy-start | bytes 24580
  208.2 18.0 %all-to-all-start.1 = ((bf16[4,2,65536]{2,1,0:T(2,128)(2,1)}), bf16[4,2,65536]{2,1,0:T(2,128)(2,1)S(1)}, u32[]{:S(2)}, u32[]{:S(2)}) async-start(bf16[4,2,65536]{2,1,0:T(2,128)(2,1)} %reshape.630), calls=%async_computation.1 | async-start | bytes 2097152 | tf_op jit(solution)/shard_map/all_to_all | solution.py:191
  212.6 74.8 %copy-start.31 = (f32[1024]{0:T(1024)}, f32[1024]{0:T(1024)S(1)}, u32[]{:S(2)}) copy-start(f32[1024]{0:T(1024)S(1)} %convert_element_type.102) | copy-start | bytes 12292
  235.7 51.8 %copy-start.12 = (f32[512,1024]{1,0:T(8,128)}, f32[512,1024]{1,0:T(8,128)S(1)}, u32[]{:S(2)}) copy-start(f32[512,1024]{1,0:T(8,128)S(1)} %get-tuple-element.454) | copy-start | bytes 6291460
  235.7 51.7 %copy-start.26 = (f32[512]{0:T(512)}, f32[512]{0:T(512)S(1)}, u32[]{:S(2)}) copy-start(f32[512]{0:T(512)S(1)} %broadcast_multiply_fusion.4) | copy-start | bytes 6148
  236.1 51.4 %copy-start.36 = (f32[512]{0:T(512)}, f32[512]{0:T(512)S(1)}, u32[]{:S(2)}) copy-start(f32[512]{0:T(512)S(1)} %add_rsqrt_fusion) | copy-start | bytes 6148
  236.1 27.8 %copy-start.18 = (bf16[1,512,1024]{2,1,0:T(8,128)(2,1)S(1)}, bf16[1,512,1024]{2,1,0:T(8,128)(2,1)}, u32[]{:S(2)}) copy-start(bf16[1,512,1024]{2,1,0:T(8,128)(2,1)} %param.31) | copy-start | bytes 3145732
  292.5 10.2 copy-start.10
  297.6 19.7 %all-to-all-start.2 = ((bf16[1,512,4,256]{3,1,0,2:T(8,128)(2,1)}), bf16[1,512,4,256]{3,1,0,2:T(8,128)(2,1)}, u32[]{:S(2)}, u32[]{:S(2)}) async-start(bf16[1,512,4,256]{3,1,0,2:T(8,128)(2,1)} %copy.79), calls=%async_computation.2 | async-start | bytes 2097152 | tf_op jit(solution)/shard_map/all_to_all | solution.py:222
  302.7 415.4 %reduce-scatter.10.cloned.1.call-start = ((), (), s32[]{:S(2)}) async-start(), calls=%async_computation.11 | async-start | bytes 4325376 | tf_op jit(solution)/shard_map/reduce_scatter | solution.py:273
  305.9 13.6 %copy-start.5 = (bf16[2048,4,64]{0,2,1:T(8,128)(2,1)S(1)}, bf16[2048,4,64]{0,2,1:T(8,128)(2,1)}, u32[]{:S(2)}) copy-start(bf16[2048,4,64]{0,2,1:T(8,128)(2,1)} %get-tuple-element.723) | copy-start | bytes 3145732
  305.9 13.6 %copy-start.8 = (bf16[2048,4,64]{0,2,1:T(8,128)(2,1)S(1)}, bf16[2048,4,64]{0,2,1:T(8,128)(2,1)}, u32[]{:S(2)}) copy-start(bf16[2048,4,64]{0,2,1:T(8,128)(2,1)} %get-tuple-element.724) | copy-start | bytes 3145732
  306.0 462.8 %reduce-scatter.8.cloned.1.call-start = ((), (), s32[]{:S(2)}) async-start(), calls=%async_computation.10 | async-start | bytes 12976128 | tf_op jit(solution)/shard_map/reduce_scatter | solution.py:272
  344.9 21.7 %copy-start.20 = (bf16[4,512,4,64]{1,3,2,0:T(8,128)(2,1)S(1)}, bf16[4,512,4,64]{1,3,2,0:T(8,128)(2,1)}, u32[]{:S(2)}) copy-start(bf16[4,512,4,64]{1,3,2,0:T(8,128)(2,1)} %get-tuple-element.689) | copy-start | bytes 3145732 | tf_op jit(solution)/shard_map/while/body/eval_jaxpr/while
  360.0 13.4 %copy-start.2 = (f32[4,512,2048]{2,1,0:T(8,128)S(1)}, f32[4,512,2048]{2,1,0:T(8,128)}, u32[]{:S(2)}) copy-start(f32[4,512,2048]{2,1,0:T(8,128)} %get-tuple-element.632) | copy-start | bytes 50331652 | tf_op jit(solution)/shard_map/while/body/eval_jaxpr/while
  402.9 22.2 %copy-start.20 = (bf16[4,512,4,64]{1,3,2,0:T(8,128)(2,1)S(1)}, bf16[4,512,4,64]{1,3,2,0:T(8,128)(2,1)}, u32[]{:S(2)}) copy-start(bf16[4,512,4,64]{1,3,2,0:T(8,128)(2,1)} %get-tuple-element.689) | copy-start | bytes 3145732 | tf_op jit(solution)/shard_map/while/body/eval_jaxpr/while
  417.9 14.0 %copy-start.2 = (f32[4,512,2048]{2,1,0:T(8,128)S(1)}, f32[4,512,2048]{2,1,0:T(8,128)}, u32[]{:S(2)}) copy-start(f32[4,512,2048]{2,1,0:T(8,128)} %get-tuple-element.632) | copy-start | bytes 50331652 | tf_op jit(solution)/shard_map/while/body/eval_jaxpr/while
  462.2 22.1 %copy-start.20 = (bf16[4,512,4,64]{1,3,2,0:T(8,128)(2,1)S(1)}, bf16[4,512,4,64]{1,3,2,0:T(8,128)(2,1)}, u32[]{:S(2)}) copy-start(bf16[4,512,4,64]{1,3,2,0:T(8,128)(2,1)} %get-tuple-element.689) | copy-start | bytes 3145732 | tf_op jit(solution)/shard_map/while/body/eval_jaxpr/while
  477.2 14.0 %copy-start.2 = (f32[4,512,2048]{2,1,0:T(8,128)S(1)}, f32[4,512,2048]{2,1,0:T(8,128)}, u32[]{:S(2)}) copy-start(f32[4,512,2048]{2,1,0:T(8,128)} %get-tuple-element.632) | copy-start | bytes 50331652 | tf_op jit(solution)/shard_map/while/body/eval_jaxpr/while
  521.4 22.1 %copy-start.20 = (bf16[4,512,4,64]{1,3,2,0:T(8,128)(2,1)S(1)}, bf16[4,512,4,64]{1,3,2,0:T(8,128)(2,1)}, u32[]{:S(2)}) copy-start(bf16[4,512,4,64]{1,3,2,0:T(8,128)(2,1)} %get-tuple-element.689) | copy-start | bytes 3145732 | tf_op jit(solution)/shard_map/while/body/eval_jaxpr/while
  536.3 14.0 %copy-start.2 = (f32[4,512,2048]{2,1,0:T(8,128)S(1)}, f32[4,512,2048]{2,1,0:T(8,128)}, u32[]{:S(2)}) copy-start(f32[4,512,2048]{2,1,0:T(8,128)} %get-tuple-element.632) | copy-start | bytes 50331652 | tf_op jit(solution)/shard_map/while/body/eval_jaxpr/while
  612.8 294.4 %reduce-scatter.6.cloned.1.call-start = ((), (), s32[]{:S(2)}) async-start(), calls=%async_computation.9 | async-start | bytes 8650752 | tf_op jit(solution)/shard_map/reduce_scatter | solution.py:270
  629.0 476.9 %reduce-scatter.12.cloned.1.call-start = ((), (), s32[]{:S(2)}) async-start(), calls=%async_computation.12 | async-start | bytes 17301504 | tf_op jit(solution)/shard_map/reduce_scatter | solution.py:275
  642.2 650.5 %reduce-scatter.14.cloned.1.call-start = ((), (), s32[]{:S(2)}) async-start(), calls=%async_computation.13 | async-start | bytes 17301504 | tf_op jit(solution)/shard_map/reduce_scatter | solution.py:277
  655.3 10.8 copy-start.30
  655.3 10.8 copy-start.35
  655.3 10.8 copy-start.41
  655.3 56.6 %copy-start.23 = (bf16[512,1024]{1,0:T(8,128)(2,1)S(1)}, bf16[512,1024]{1,0:T(8,128)(2,1)}, u32[]{:S(2)}) copy-start(bf16[512,1024]{1,0:T(8,128)(2,1)} %copy-done.22) | copy-start | bytes 3145732
  711.9 580.8 %copy-start.1 = (bf16[1024,1024]{1,0:T(8,128)(2,1)S(1)}, bf16[1024,1024]{1,0:T(8,128)(2,1)}, u32[]{:S(2)}) copy-start(bf16[1024,1024]{1,0:T(8,128)(2,1)} %param.25) | copy-start | bytes 6291460
  (43 other events, 170.3 us)
Sparse Core Ops, SparseCore 0:
  306.4 126.9 reduce-scatter.9
  612.9 155.8 reduce-scatter.7
  771.8 135.4 reduce-scatter.5
  910.1 195.8 reduce-scatter.11
  1108.8 183.8 reduce-scatter.13
